TPU v7x, 32 devices: a whole 2x2x4 slice. The times are simulated.
32 devices in a mesh: gx: 4 (over z), gy: 2 (over x), gz: 4 (over y, core).
Axes of the slice: x: 2, y: 2, z: 4, core: 2. Of those that a mesh axis runs over, the one named last changes fastest.
Arguments:
- initial_field: float32 [3, 32, 64, 512], P(None, 'gx', 'gy', 'gz'), may hold values from -6 to 6
- inv_permittivity: float32 [32, 64, 512], P('gx', 'gy', 'gz'), may hold values from 0.25 to 1
- history: bfloat16 [768, 12, 256], P(('gx', 'gy', 'gz')), may hold values from -6 to 6
- tile_rows: int32 [768], P(('gx', 'gy', 'gz')), may hold values from 0 to 255
- owners: int32 [768, 1], P(('gx', 'gy', 'gz')), may hold values from 0 to 3; in each aligned block of 24 rows (0 to 23, 24 to 47, ...) at most 12 rows name the same one
- delays: int32 [768, 4096], P(('gx', 'gy', 'gz')), may hold values from 0 to 3
- weights: bfloat16 [256, 4096], replicated, may hold values from -0.375 to 0.375
Outputs:
- efield: float32 [3, 32, 64, 512], P(None, 'gx', 'gy', 'gz')
- far_field: float32 [4, 20, 4096], P('gx', None, ('gy', 'gz'))
Inputs may be any that keep to these rules, and one draw needn't show every extreme that they name: `owners`: among the 24 tiles of one device no section is named more than 12 times, a bound that some block reaches.
All inputs are finite; a program needn't handle non-finite values.
Results may differ from a plain program's by a relative error of at most 0.0014.
Values may be sent and summed in bfloat16 or wider, within the bound.
A program may use at most 128 MiB of HBM per device.

v0:
```python
import functools

import jax
import jax.numpy as jnp
from jax import lax
from jax.experimental import pallas as pl
from jax.experimental.pallas import tpu as pltpu
from jax.sharding import PartitionSpec as P

STEPS = 4
LAG = 4
NB = 20

courant = 0.5
MESH = pl.DeviceIdType.MESH
WIDE = 256


def kernel(
    dims,
    field_ref, perm_ref, hist_ref, rows_ref, owners_ref, delays_hbm, weights_hbm,
    eout_ref, far_ref,
    e, h, perm, delays_ref, weights_ref,
    xs, ys, zs, xt, yt, zt,
    xr, yr, zr, xl, yl, zl, exz, eyz, exy, ezy, eyx, ezx,
    hxm, hym, hzm,
    placed_past, placed_new, placed_delay, proj,
    part_old, part_new, recv_a_old, recv_a_new, sum_a_old, sum_a_new,
    recv_b_old, recv_b_new, sum_b_old, sum_b_new, recv_c_old, recv_c_new,
    hs_sem, hr_sem, a_send, a_recv, b_send, b_recv, c_send, c_recv, in_sem,
):
    n_x, n_y, n_z, sx, sy, sz, tiles, hpast, cap, old_rows, new_rows, share = dims
    gx, gy, gz = lax.axis_index("gx"), lax.axis_index("gy"), lax.axis_index("gz")
    core, plane_z = gz % 2, gz // 2
    plane_n = n_y * (n_z // 2)
    plane_me = gy * (n_z // 2) + plane_z
    slots = n_x * cap
    wide_rows = max(8, n_x)
    groups = slots // wide_rows
    members = n_y * n_z

    loads = [
        pltpu.make_async_copy(source, target, in_sem.at[i])
        for i, (source, target) in enumerate(
            ((field_ref, e), (perm_ref, perm), (delays_hbm, delays_ref), (weights_hbm, weights_ref))
        )
    ]
    store_e = pltpu.make_async_copy(e, eout_ref, in_sem.at[len(loads)])
    for load in loads:
        load.start()

    for ref in (xr, yr, zr, xl, yl, zl, exz, eyz, exy, ezy, eyx, ezx):
        ref[...] = jnp.zeros_like(ref)

    barrier = pltpu.get_barrier_semaphore()
    for j in range(1, n_x):
        pl.semaphore_signal(barrier, inc=1, device_id=((gx + j) % n_x, gy, gz), device_id_type=MESH)
    member_me = gy * n_z + gz
    for j in range(1, members):
        other = (member_me + j) % members
        pl.semaphore_signal(
            barrier, inc=1, device_id=(gx, other // n_z, other % n_z), device_id_type=MESH
        )

    tail = slice(sy - 8, sy)
    copies = (
        ((-1, 0, 0), lambda k: xs.at[k], lambda k: xr.at[k]),
        ((1, 0, 0), lambda k: xt.at[k], lambda k: xl.at[k]),
        ((1, 0, -1), lambda k: zs.at[k], lambda k: exz.at[k]),
        ((-1, 0, 1), lambda k: xs.at[k, 1], lambda k: ezx.at[k]),
        ((1, -1, 0), lambda k: ys.at[k], lambda k: exy.at[k]),
        ((-1, 1, 0), lambda k: xs.at[k, 0, tail], lambda k: eyx.at[k]),
        ((0, 1, -1), lambda k: zs.at[k, tail], lambda k: eyz.at[k]),
        ((0, -1, 1), lambda k: ys.at[k], lambda k: ezy.at[k]),
        ((0, -1, 0), lambda k: ys.at[k], lambda k: yr.at[k]),
        ((0, 1, 0), lambda k: yt.at[k], lambda k: yl.at[k]),
        ((0, 0, -1), lambda k: zs.at[k], lambda k: zr.at[k]),
        ((0, 0, 1), lambda k: zt.at[k], lambda k: zl.at[k]),
    )

    def at_offset(offset, sign):
        inside, place = None, []
        for pos, count, step in zip((gx, gy, gz), (n_x, n_y, n_z), offset):
            step = sign * step
            if step:
                fits = (pos > 0) if step < 0 else (pos < count - 1)
                inside = fits if inside is None else jnp.logical_and(inside, fits)
            place.append(jnp.clip(pos + step, 0, count - 1) if step else pos)
        return inside, tuple(place)

    diagonals = ((1, 0, -1), (-1, 0, 1), (1, -1, 0), (-1, 1, 0))
    for ox, oy, oz in diagonals:
        target = ((gx + ox + n_x) % n_x, (gy + oy + n_y) % n_y, (gz + oz + n_z) % n_z)
        pl.semaphore_signal(barrier, inc=1, device_id=target, device_id_type=MESH)

    lane = lax.broadcasted_iota(jnp.int32, (sy, sz), 1)
    row = lax.broadcasted_iota(jnp.int32, (sy, sz), 0)

    def stage(slot):
        for i, c in enumerate((1, 2)):
            xs[slot, i] = e[c, 0]
        for c in range(3):
            xt[slot, c] = e[c, sx - 1]
        for i, c in enumerate((0, 2)):
            for x in range(sx):
                ys[slot, i, x : x + 1, :] = e[c, x, 0:1, :]
        for c in range(3):
            for x in range(sx):
                yt[slot, c, x : x + 1, :] = e[c, x, sy - 1 : sy, :]
        low = jnp.zeros((sy, sz), jnp.float32)
        high = jnp.zeros((sy, sz), jnp.float32)
        for c in range(3):
            for x in range(sx):
                at = c * sx + x
                if c < 2:
                    low = jnp.where(lane == at, pltpu.roll(e[c, x], at, 1), low)
                high = jnp.where(lane == at, pltpu.roll(e[c, x], at + 1, 1), high)
        zs[slot] = low
        zt[slot] = high

    def halo_copy(slot, number):
        offset, source, target = copies[number]
        return pltpu.make_async_remote_copy(
            src_ref=source(slot), dst_ref=target(slot),
            send_sem=hs_sem.at[slot, number], recv_sem=hr_sem.at[slot, number],
            device_id=at_offset(offset, 1)[1], device_id_type=MESH,
        )

    def send_halo(slot):
        for number in range(len(copies)):
            @pl.when(at_offset(copies[number][0], 1)[0])
            def _():
                halo_copy(slot, number).start()

    def wait_halo(slot):
        for number in range(len(copies)):
            @pl.when(at_offset(copies[number][0], -1)[0])
            def _():
                halo_copy(slot, number).wait_recv()

    def end_halo(slot):
        for number in range(len(copies)):
            @pl.when(at_offset(copies[number][0], 1)[0])
            def _():
                halo_copy(slot, number).wait_send()

    def next_y(v, slot, i, x, low):
        if low:
            return jnp.where(row == 0, hym[i, x : x + 1, :], pltpu.roll(v, 1, 0))
        return jnp.where(row == sy - 1, yr[slot, i, x : x + 1, :], pltpu.roll(v, sy - 1, 0))

    def next_z(v, c, x, packed, low):
        if low:
            return jnp.where(
                lane == 0, pltpu.roll(hzm[c], (sz - x) % sz, 1), pltpu.roll(v, 1, 1)
            )
        at = c * sx + x
        return jnp.where(
            lane == sz - 1, pltpu.roll(packed, (sz - 1 - at) % sz, 1), pltpu.roll(v, sz - 1, 1)
        )

    def next_x(ref, slot, i, c, x, low):
        if low:
            return ref[c, x - 1] if x > 0 else hxm[i]
        return ref[c, x + 1] if x < sx - 1 else xr[slot, i]

    lane8 = lax.broadcasted_iota(jnp.int32, (sx, sz), 1)
    row8 = lax.broadcasted_iota(jnp.int32, (sx, sz), 0)

    def update_below(slot, first):
        def put(ref, i, change, exists):
            fresh = -change if first else ref[i] - change
            ref[i] = jnp.where(exists, fresh, 0.0)

        ex, ey, ez = xl[slot, 0], xl[slot, 1], xl[slot, 2]
        ex_z = jnp.where(
            lane == sz - 1, pltpu.roll(exz[slot], sz - sx, 1), pltpu.roll(ex, sz - 1, 1)
        )
        ex_y = jnp.where(row == sy - 1, exy[slot, 0, sx - 1 : sx, :], pltpu.roll(ex, sy - 1, 0))
        put(hxm, 0, courant * ((ex_z - ex) - (xs[slot, 1] - ez)), gx > 0)
        put(hxm, 1, courant * ((xs[slot, 0] - ey) - (ex_y - ex)), gx > 0)

        ex, ey, ez = yl[slot, 0], yl[slot, 1], yl[slot, 2]
        edge = jnp.sum(
            jnp.where(lane8 == row8 + sx, jnp.broadcast_to(eyz[slot, 7:8, :], (sx, sz)), 0.0),
            axis=1, keepdims=True,
        )
        ey_z = jnp.where(lane8 == sz - 1, edge, pltpu.roll(ey, sz - 1, 1))
        ey_x = jnp.where(row8 == sx - 1, eyx[slot, 7:8, :], pltpu.roll(ey, sx - 1, 0))
        put(hym, 0, courant * ((ys[slot, 1] - ez) - (ey_z - ey)), gy > 0)
        put(hym, 1, courant * ((ey_x - ey) - (ys[slot, 0] - ex)), gy > 0)

        ex = zl[slot]
        ey = pltpu.roll(ex, sz - sx, 1)
        ez = pltpu.roll(ex, sz - 2 * sx, 1)
        ex_up = zs[slot]
        ey_up = pltpu.roll(ex_up, sz - sx, 1)
        column = jnp.sum(jnp.where(lane8 == sz - 1, ezy[slot, 1], 0.0), axis=1, keepdims=True)
        edge = jnp.sum(jnp.where(lane8 == row8, column, 0.0), axis=0, keepdims=True)
        ez_y = jnp.where(row == sy - 1, edge, pltpu.roll(ez, sy - 1, 0))
        ez_x = jnp.where(lane == sx - 1, pltpu.roll(ezx[slot], sx, 1), pltpu.roll(ez, sz - 1, 1))
        put(hzm, 0, courant * ((ez_y - ez) - (ey_up - ey)), gz > 0)
        put(hzm, 1, courant * ((ex_up - ex) - (ez_x - ez)), gz > 0)

    def update_h(slot, first):
        packed = zr[slot]
        for x in range(sx):
            ex, ey, ez = e[0, x], e[1, x], e[2, x]
            ez_y, ex_y = next_y(ez, slot, 1, x, False), next_y(ex, slot, 0, x, False)
            ey_z, ex_z = next_z(ey, 1, x, packed, False), next_z(ex, 0, x, packed, False)
            ez_x, ey_x = next_x(e, slot, 1, 2, x, False), next_x(e, slot, 0, 1, x, False)
            changes = (
                courant * ((ez_y - ez) - (ey_z - ey)),
                courant * ((ex_z - ex) - (ez_x - ez)),
                courant * ((ey_x - ey) - (ex_y - ex)),
            )
            for c in range(3):
                h[c, x] = -changes[c] if first else h[c, x] - changes[c]

    def update_e(slot):
        for x in range(sx):
            hx, hy, hz = h[0, x], h[1, x], h[2, x]
            hz_y, hx_y = next_y(hz, slot, 1, x, True), next_y(hx, slot, 0, x, True)
            hy_z, hx_z = next_z(hy, 1, x, None, True), next_z(hx, 0, x, None, True)
            hz_x, hy_x = next_x(h, slot, 1, 2, x, True), next_x(h, slot, 0, 1, x, True)
            scale = courant * perm[x]
            e[0, x] = e[0, x] + scale * ((hz - hz_y) - (hy - hy_z))
            e[1, x] = e[1, x] + scale * ((hx - hx_z) - (hz - hz_x))
            e[2, x] = e[2, x] + scale * ((hy - hy_x) - (hx - hx_y))

    loads[0].wait()
    stage(0)

    owner_row = owners_ref[...]
    ti = lax.broadcasted_iota(jnp.int32, (tiles, tiles), 0)
    tj = lax.broadcasted_iota(jnp.int32, (tiles, tiles), 1)
    owner_wide = jnp.broadcast_to(owner_row, (tiles, tiles))
    owner_col = jnp.sum(jnp.where(ti == tj, owner_wide, 0), axis=1, keepdims=True)
    rank_row = jnp.sum(
        jnp.where((owner_col == owner_wide) & (ti < tj), 1, 0), axis=0, keepdims=True
    )
    slot_row = rank_row * n_x + owner_row
    slot_ids = lax.broadcasted_iota(jnp.int32, (slots, tiles), 0)
    place = jnp.where(slot_ids == slot_row, 1.0, 0.0).astype(jnp.bfloat16)
    pick = jnp.where(
        lax.broadcasted_iota(jnp.int32, (sx * sy, tiles), 0) == rows_ref[...], 1.0, 0.0
    ).astype(jnp.bfloat16)
    sampler = lax.dot_general(
        place, pick, (((1,), (1,)), ((), ())), preferred_element_type=jnp.float32
    ).astype(jnp.bfloat16)

    pl.semaphore_wait(barrier, n_x - 1 + members - 1 + len(diagonals))
    send_halo(0)

    for t in range(hpast):
        placed_past[t * slots : (t + 1) * slots, :] = jnp.dot(
            place, hist_ref[t], preferred_element_type=jnp.float32
        ).astype(jnp.bfloat16)
    loads[1].wait()
    loads[2].wait()
    placed_delay[...] = jnp.dot(
        place, delays_ref[...].astype(jnp.float32).astype(jnp.bfloat16),
        preferred_element_type=jnp.float32,
    )
    loads[3].wait()

    def project(source, time0, times, part, pad_rows, add, parity, first, count):
        per = share // WIDE

        def body(i, carry):
            member = 2 * (i // per) + parity
            start = pl.multiple_of(member * share + (i % per) * WIDE, WIDE)
            proj[0 : times * slots, :] = jnp.dot(
                source[time0 * slots : (time0 + times) * slots, :], weights_ref[:, pl.ds(start, WIDE)],
                preferred_element_type=jnp.float32,
            )
            for q in range(WIDE // 128):
                column = pl.multiple_of(start + q * 128, 128)
                inside = (i % per) * (WIDE // 128) + q
                for block in range(wide_rows // 8):
                    bins = [None] * (time0 + times + LAG - 1)
                    for g in range(groups):
                        base = g * wide_rows + block * 8
                        late = placed_delay[base : base + 8, pl.ds(column, 128)]
                        keeps = [late == float(lag) for lag in range(LAG)]
                        for t in range(times):
                            value = proj[t * slots + base : t * slots + base + 8, q * 128 : q * 128 + 128]
                            for lag in range(LAG):
                                piece = jnp.where(keeps[lag], value, 0.0)
                                b = time0 + t + lag
                                bins[b] = piece if bins[b] is None else bins[b] + piece
                    bins = bins + [None] * (pad_rows - len(bins))
                    for b in range(pad_rows):
                        if bins[b] is None:
                            if add:
                                continue
                            bins[b] = jnp.zeros((8, 128), jnp.float32)
                        if n_x >= 8:
                            kept, many = bins[b], 8
                        else:
                            kept, many = bins[b][0:n_x], n_x
                            for other in range(n_x, 8, n_x):
                                kept = kept + bins[b][other : other + n_x]
                        spot = pl.ds(block * 8 * pad_rows + b, many, stride=pad_rows)
                        if add:
                            kept = kept + part[member, inside, spot, :]
                        part[member, inside, spot, :] = kept
            return carry

        lax.fori_loop(first, first + count, body, 0)

    sets = (
        (part_old, recv_a_old, sum_a_old, recv_b_old, sum_b_old, recv_c_old, old_rows),
        (part_new, recv_a_new, sum_a_new, recv_b_new, sum_b_new, recv_c_new, new_rows),
    )

    def copy_a(which, m):
        part, recv = sets[which][0], sets[which][1]
        other = 1 - core
        return pltpu.make_async_remote_copy(
            src_ref=part.at[2 * m + other], dst_ref=recv.at[m],
            send_sem=a_send.at[which, m], recv_sem=a_recv.at[which, m],
            device_id=(gx, gy, plane_z * 2 + other), device_id_type=MESH,
        )

    blocks = share // 128
    cuts = ((0, blocks // 2, blocks), (0, blocks))

    def copy_b(which, piece, j):
        span = slice(cuts[which][piece], cuts[which][piece + 1])
        summed, recv = sets[which][2], sets[which][3]
        other = (plane_me + j) % plane_n
        half = n_z // 2
        return pltpu.make_async_remote_copy(
            src_ref=summed.at[other, span], dst_ref=recv.at[j, span],
            send_sem=b_send.at[2 * which + piece, j], recv_sem=b_recv.at[2 * which + piece, j],
            device_id=(gx, other // half, (other % half) * 2 + core), device_id_type=MESH,
        )

    def copy_c(which, j):
        summed, recv, rows = sets[which][4], sets[which][5], sets[which][6]
        other = (gx + j) % n_x
        return pltpu.make_async_remote_copy(
            src_ref=summed.at[:, pl.ds(pl.multiple_of(other * rows, 8), rows)], dst_ref=recv.at[j],
            send_sem=c_send.at[which, j], recv_sem=c_recv.at[which, j],
            device_id=(other, gy, gz), device_id_type=MESH,
        )

    def begin_a(which):
        for m in range(plane_n):
            copy_a(which, m).start()

    def a_to_b(which):
        part, recv, summed = sets[which][0], sets[which][1], sets[which][2]
        for j in list(range(1, plane_n)) + [0]:
            m = (plane_me + j) % plane_n
            copy_a(which, m).wait_recv()
            summed[m] = part[2 * m + core] + recv[m]
            if j > 0:
                copy_b(which, 0, j).start()

    def b_to_c(which):
        total = sets[which][2][plane_me]
        for j in range(1, plane_n):
            for piece in range(len(cuts[which]) - 1):
                copy_b(which, piece, j).wait_recv()
            total = total + sets[which][3][j]
        sets[which][4][...] = total
        for j in range(1, n_x):
            copy_c(which, j).start()

    def end_c(which):
        rows = sets[which][6]
        total = sets[which][4][:, pl.ds(pl.multiple_of(gx * rows, 8), rows), :]
        for j in range(1, n_x):
            copy_c(which, j).wait_recv()
            total = total + sets[which][5][j]
        for m in range(plane_n):
            copy_a(which, m).wait_send()
        for j in range(1, plane_n):
            for piece in range(len(cuts[which]) - 1):
                copy_b(which, piece, j).wait_send()
        for j in range(1, n_x):
            copy_c(which, j).wait_send()
        return total

    chunks = plane_n * share // WIDE
    other = 1 - core

    def sample(step):
        for m in range(2):
            flat = h[m].reshape(sx * sy, sz).astype(jnp.bfloat16)
            placed_new[step * slots : (step + 1) * slots, m * sz : (m + 1) * sz] = jnp.dot(
                sampler, flat, preferred_element_type=jnp.float32
            ).astype(jnp.bfloat16)

    def past(parity, first, count):
        project(placed_past, 0, hpast, part_old, old_rows, False, parity, first, count)

    def early(parity, first, count):
        project(placed_new, 0, STEPS - 1, part_new, new_rows, False, parity, first, count)

    def last(parity):
        project(placed_new, STEPS - 1, 1, part_new, new_rows, True, parity, 0, chunks)

    def beside(step):
        if step == 0:
            past(other, 0, chunks)
            begin_a(0)
            past(core, 0, chunks)
        elif step == 1:
            a_to_b(0)
        elif step == 2:
            for j in range(1, plane_n):
                copy_b(0, 1, j).start()
        elif step == 3:
            early(other, 0, chunks)
            early(core, 0, chunks)
            b_to_c(0)

    for step in range(STEPS):
        beside(step)
        wait_halo(step)
        update_h(step, step == 0)
        if step < STEPS - 1:
            update_below(step, step == 0)
            update_e(step)
            stage(step + 1)
            send_halo(step + 1)
            sample(step)
        else:
            sample(step)
            last(other)
            begin_a(1)
            last(core)
            update_below(step, False)
            update_e(step)
    store_e.start()
    a_to_b(1)
    scale = float(tiles * members) ** (-0.5)
    old = end_c(0)
    for step in range(STEPS):
        end_halo(step)
    b_to_c(1)
    far_ref[...] = jnp.zeros_like(far_ref)
    new = end_c(1)
    used = min(new_rows, NB - hpast)
    for q in range(share // 128):
        columns = slice(q * 128, q * 128 + 128)
        far_ref[0:old_rows, columns] = old[q] * scale
        far_ref[hpast : hpast + used, columns] = (
            far_ref[hpast : hpast + used, columns] + (new[q] * scale)[0:used]
        )
    store_e.wait()


def up8(n):
    return (n + 7) // 8 * 8


def local(sizes, initial_field, inv_permittivity, history, tile_rows, owners, delays, weights):
    n_x, n_y, n_z = sizes
    sx, sy, sz = inv_permittivity.shape
    tiles, hpast, width = history.shape
    cap = max(2, 2 * tiles // n_x)
    slots = n_x * cap
    members = n_y * n_z
    plane_n = n_y * (n_z // 2)
    directions = weights.shape[1]
    share = directions // members
    old_rows, new_rows = up8(hpast + LAG - 1), up8(STEPS + LAG - 1)
    dims = (n_x, n_y, n_z, sx, sy, sz, tiles, hpast, cap, old_rows, new_rows, share)
    anywhere, resident = pl.BlockSpec(memory_space=pl.ANY), pl.BlockSpec(memory_space=pltpu.VMEM)
    f32, bf16 = jnp.float32, jnp.bfloat16
    vmem = pltpu.VMEM
    faces = lambda low: [
        vmem((STEPS, low, sy, sz), f32), vmem((STEPS, low, sx, sz), f32), vmem((STEPS, sy, sz), f32)
    ]
    flat, rows8 = vmem((STEPS, sy, sz), f32), vmem((STEPS, 8, sz), f32)
    edges = [flat, rows8] + [vmem((STEPS, 2, sx, sz), f32)] * 2 + [rows8, flat]
    below = [vmem((2, sy, sz), f32), vmem((2, sx, sz), f32), vmem((2, sy, sz), f32)]
    per_set = lambda make: [make(n_x * old_rows, old_rows), make(n_x * new_rows, new_rows)]
    scratch = (
        [vmem((3, sx, sy, sz), f32), vmem((3, sx, sy, sz), f32), vmem((sx, sy, sz), f32)]
        + [vmem(delays.shape, jnp.int32), vmem(weights.shape, bf16)]
        + faces(2)
        + faces(3)
        + faces(2)
        + faces(3)
        + edges
        + below
        + [
            vmem((hpast * slots, width), bf16),
            vmem((STEPS * slots, width), bf16),
            vmem((slots, directions), f32),
            vmem((max(hpast, STEPS) * slots, WIDE), f32),
        ]
        + per_set(lambda rows, one: vmem((members, share // 128, rows, 128), f32))
        + per_set(lambda rows, one: vmem((plane_n, share // 128, rows, 128), f32))
        + per_set(lambda rows, one: vmem((plane_n, share // 128, rows, 128), f32))
        + per_set(lambda rows, one: vmem((plane_n, share // 128, rows, 128), f32))
        + per_set(lambda rows, one: vmem((share // 128, rows, 128), f32))
        + per_set(lambda rows, one: vmem((n_x, share // 128, one, 128), f32))
        + [pltpu.SemaphoreType.DMA((STEPS, 12))] * 2
        + [pltpu.SemaphoreType.DMA((2, plane_n))] * 2
        + [pltpu.SemaphoreType.DMA((3, plane_n))] * 2
        + [pltpu.SemaphoreType.DMA((2, n_x))] * 2
        + [pltpu.SemaphoreType.DMA((5,))]
    )
    efield, far = pl.pallas_call(
        functools.partial(kernel, dims),
        out_shape=(
            jax.ShapeDtypeStruct(initial_field.shape, f32),
            jax.ShapeDtypeStruct((NB, share), f32),
        ),
        in_specs=[anywhere] * 2 + [resident] * 3 + [anywhere] * 2,
        out_specs=(anywhere, resident),
        scratch_shapes=scratch,
        compiler_params=pltpu.CompilerParams(
            collective_id=0, has_side_effects=True, vmem_limit_bytes=62 * 1024 * 1024
        ),
    )(
        initial_field, inv_permittivity, jnp.transpose(history, (1, 0, 2)),
        tile_rows[None], owners.reshape(1, tiles), delays, weights,
    )
    return (efield, far[None])


def solution(mesh):
    placed = (
        P(None, "gx", "gy", "gz"),
        P("gx", "gy", "gz"),
        P(("gx", "gy", "gz"), None, None),
        P(("gx", "gy", "gz")),
        P(("gx", "gy", "gz"), None),
        P(("gx", "gy", "gz"), None),
        P(),
    )
    sizes = (mesh.shape["gx"], mesh.shape["gy"], mesh.shape["gz"])
    return jax.shard_map(
        functools.partial(local, sizes),
        mesh=mesh,
        in_specs=placed,
        out_specs=(P(None, "gx", "gy", "gz"), P("gx", None, ("gy", "gz"))),
        check_vma=False,
    )
```

profile of v0, /device:TPU:0, one launch (start us, length us, event | category | flops | bytes accessed | tf_op | source)
XLA Modules:
  0.0 43.8 jit_solution(2900513107439512738)
XLA Ops:
  0.6 39.9 %shard_map.86 = (f32[3,8,32,128]{3,2,1,0:T(8,128)}, f32[20,512]{1,0:T(8,128)}) custom-call(f32[3,8,32,128]{3,2,1,0:T(8,128)} %field_ref.1, f32[8,32,128]{2,1,0:T(8,128)} %perm_ref.1, bf16[12,24,256]{2,1,0:T(8,128)(2,1)} %bitcast.4, s32[1,24]{1,0:T(1,128)} %bitcast.6, s32[1,24]{1,0:T(1,128)} %bitcast.7, s32[24,4096]{1,0:T(8,128)} %delays_hbm.1, ...), custom_call_target="tpu_custom_call" | custom-call | tf_op jit(solution)/shard_map/pallas_call | solution.py:510
  40.5 1.5 %copy.9 = f32[1,20,512]{2,0,1:T(1,128)} copy(f32[1,20,512]{2,1,0:T(8,128)} %bitcast.5) | data formatting | bytes 81920
  42.0 1.8 %copy.11 = f32[3,8,32,128]{3,2,1,0:T(8,128)} copy(f32[3,8,32,128]{3,2,1,0:T(8,128)} %get-tuple-element.10) | data formatting | bytes 786432
where the time goes:
time: 44 us; the launch traced here: 43.8 us
  Pallas kernels  39.9 us (91%)
  local copies, waits for them, and re-layouts  3.22 us (7%)
  between operations  0.64 us (1%)
    pallas_call x1, Pallas kernels, local(): pl.pallas_call(functools.partial(kernel, dims), out_shape=(jax.ShapeDtype...  39.9 us
    unnamed x2, local copies, waits for them, and re-layouts  3.22 us

commit v1 on v0

--- a/solution.py
+++ b/solution.py
@@ -18,9 +18,9 @@
 
 def kernel(
     dims,
-    field_ref, perm_ref, hist_ref, rows_ref, owners_ref, delays_hbm, weights_hbm,
-    eout_ref, far_ref,
-    e, h, perm, delays_ref, weights_ref,
+    field_ref, perm_ref, hist_hbm, rows_hbm, owners_hbm, delays_hbm, weights_hbm,
+    e, far_ref,
+    h, perm, hist_ref, rows_ref, owners_ref, delays_ref, weights_ref,
     xs, ys, zs, xt, yt, zt,
     xr, yr, zr, xl, yl, zl, exz, eyz, exy, ezy, eyx, ezx,
     hxm, hym, hzm,
@@ -42,10 +42,12 @@
     loads = [
         pltpu.make_async_copy(source, target, in_sem.at[i])
         for i, (source, target) in enumerate(
-            ((field_ref, e), (perm_ref, perm), (delays_hbm, delays_ref), (weights_hbm, weights_ref))
+            (
+                (field_ref, e), (owners_hbm, owners_ref), (rows_hbm, rows_ref), (hist_hbm, hist_ref),
+                (delays_hbm, delays_ref), (perm_ref, perm), (weights_hbm, weights_ref),
+            )
         )
     ]
-    store_e = pltpu.make_async_copy(e, eout_ref, in_sem.at[len(loads)])
     for load in loads:
         load.start()
 
@@ -231,6 +233,8 @@
     loads[0].wait()
     stage(0)
 
+    loads[1].wait()
+    loads[2].wait()
     owner_row = owners_ref[...]
     ti = lax.broadcasted_iota(jnp.int32, (tiles, tiles), 0)
     tj = lax.broadcasted_iota(jnp.int32, (tiles, tiles), 1)
@@ -252,17 +256,18 @@
     pl.semaphore_wait(barrier, n_x - 1 + members - 1 + len(diagonals))
     send_halo(0)
 
+    loads[3].wait()
     for t in range(hpast):
         placed_past[t * slots : (t + 1) * slots, :] = jnp.dot(
             place, hist_ref[t], preferred_element_type=jnp.float32
         ).astype(jnp.bfloat16)
-    loads[1].wait()
-    loads[2].wait()
+    loads[4].wait()
     placed_delay[...] = jnp.dot(
         place, delays_ref[...].astype(jnp.float32).astype(jnp.bfloat16),
         preferred_element_type=jnp.float32,
     )
-    loads[3].wait()
+    loads[5].wait()
+    loads[6].wait()
 
     def project(source, time0, times, part, pad_rows, add, parity, first, count):
         per = share // WIDE
@@ -435,7 +440,6 @@
             last(core)
             update_below(step, False)
             update_e(step)
-    store_e.start()
     a_to_b(1)
     scale = float(tiles * members) ** (-0.5)
     old = end_c(0)
@@ -451,7 +455,17 @@
         far_ref[hpast : hpast + used, columns] = (
             far_ref[hpast : hpast + used, columns] + (new[q] * scale)[0:used]
         )
-    store_e.wait()
+
+
+def store_kernel(e_ref, far_ref, eout_ref, fout_ref, sem):
+    bins = far_ref.shape[0]
+    stores = [pltpu.make_async_copy(e_ref, eout_ref, sem.at[bins])] + [
+        pltpu.make_async_copy(far_ref.at[b : b + 1], fout_ref.at[b], sem.at[b]) for b in range(bins)
+    ]
+    for store in stores:
+        store.start()
+    for store in stores:
+        store.wait()
 
 
 def up8(n):
@@ -481,7 +495,8 @@
     below = [vmem((2, sy, sz), f32), vmem((2, sx, sz), f32), vmem((2, sy, sz), f32)]
     per_set = lambda make: [make(n_x * old_rows, old_rows), make(n_x * new_rows, new_rows)]
     scratch = (
-        [vmem((3, sx, sy, sz), f32), vmem((3, sx, sy, sz), f32), vmem((sx, sy, sz), f32)]
+        [vmem((3, sx, sy, sz), f32), vmem((sx, sy, sz), f32)]
+        + [vmem((hpast, tiles, width), bf16), vmem((1, tiles), jnp.int32), vmem((1, tiles), jnp.int32)]
         + [vmem(delays.shape, jnp.int32), vmem(weights.shape, bf16)]
         + faces(2)
         + faces(3)
@@ -505,25 +520,33 @@
         + [pltpu.SemaphoreType.DMA((2, plane_n))] * 2
         + [pltpu.SemaphoreType.DMA((3, plane_n))] * 2
         + [pltpu.SemaphoreType.DMA((2, n_x))] * 2
-        + [pltpu.SemaphoreType.DMA((5,))]
+        + [pltpu.SemaphoreType.DMA((7,))]
     )
     efield, far = pl.pallas_call(
         functools.partial(kernel, dims),
-        out_shape=(
-            jax.ShapeDtypeStruct(initial_field.shape, f32),
-            jax.ShapeDtypeStruct((NB, share), f32),
-        ),
-        in_specs=[anywhere] * 2 + [resident] * 3 + [anywhere] * 2,
-        out_specs=(anywhere, resident),
+        out_shape=(vmem(initial_field.shape, f32), vmem((NB, share), f32)),
+        in_specs=[anywhere] * 7,
+        out_specs=(resident, resident),
         scratch_shapes=scratch,
         compiler_params=pltpu.CompilerParams(
-            collective_id=0, has_side_effects=True, vmem_limit_bytes=62 * 1024 * 1024
+            collective_id=0, has_side_effects=True, vmem_limit_bytes=56 * 1024 * 1024
         ),
     )(
         initial_field, inv_permittivity, jnp.transpose(history, (1, 0, 2)),
         tile_rows[None], owners.reshape(1, tiles), delays, weights,
     )
-    return (efield, far[None])
+    efield = pltpu.with_memory_space_constraint(efield, pltpu.VMEM)
+    far = pltpu.with_memory_space_constraint(far, pltpu.VMEM)
+    efield, far = pl.pallas_call(
+        store_kernel,
+        out_shape=(
+            jax.ShapeDtypeStruct(initial_field.shape, f32), jax.ShapeDtypeStruct((NB, 1, share), f32)
+        ),
+        in_specs=[resident, resident],
+        out_specs=(anywhere, anywhere),
+        scratch_shapes=[pltpu.SemaphoreType.DMA((NB + 1,))],
+    )(efield, far)
+    return efield, jnp.transpose(far, (1, 0, 2))
 
 
 def solution(mesh):

time: 44 us -> 40.1 us (0.911)
  local copies, waits for them, and re-layouts: 3.22 us -> 0 us
  Pallas kernels: 39.9 us -> 39.3 us
    unnamed x2 -> x0, local copies, waits for them, and re-layouts: 3.22 us -> none
    pallas_call x1 -> x2, Pallas kernels: 39.9 us -> 39.3 us  [the longest x1 38.4 us: local(): pl.pallas_call(functools.partial(kernel, dims), out_shape=(vmem(initial_f...]
where the time goes in v1:
time: 40.1 us; the launch traced here: 40 us
  Pallas kernels  39.3 us (98%)
  between operations  0.64 us (2%)
    pallas_call x1, Pallas kernels, local(): pl.pallas_call(functools.partial(kernel, dims), out_shape=(vmem(initial_f...  38.4 us
    pallas_call x1, Pallas kernels, local(): pl.pallas_call(store_kernel, out_shape=(jax.ShapeDtypeStruct(initial_fiel...  0.97 us

profile of v1, /device:TPU:0, one launch (start us, length us, event | category | flops | bytes accessed | tf_op | source)
XLA Modules:
  0.0 40.0 jit_solution(11505071326310742292)
XLA Ops:
  0.6 38.4 %shard_map.86 = (f32[3,8,32,128]{3,2,1,0:T(8,128)S(1)}, f32[20,512]{1,0:T(8,128)S(1)}) custom-call(f32[3,8,32,128]{3,2,1,0:T(8,128)} %field_ref.1, f32[8,32,128]{2,1,0:T(8,128)} %perm_ref.1, bf16[12,24,256]{2,1,0:T(8,128)(2,1)} %bitcast.4, s32[1,24]{1,0:T(1,128)} %bitcast.5, s32[1,24]{1,0:T(1,128)} %bitcast.6, s32[24,4096]{1,0:T(8,128)} %delays_hbm.1, ...), custom_call_target="tpu_custom_call" | custom-call | tf_op jit(solution)/shard_map/pallas_call | solution.py:525
  39.0 1.0 %shard_map.87 = (f32[3,8,32,128]{3,2,1,0:T(8,128)}, f32[20,1,512]{2,1,0:T(1,128)}) custom-call(f32[3,8,32,128]{3,2,1,0:T(8,128)S(1)} %get-tuple-element.6.e_ref, f32[20,512]{1,0:T(8,128)S(1)} %get-tuple-element.7.far_ref), custom_call_target="tpu_custom_call" | custom-call | tf_op jit(solution)/shard_map/pallas_call | solution.py:540

commit v2 on v1

--- a/solution.py
+++ b/solution.py
@@ -24,12 +24,13 @@
     xs, ys, zs, xt, yt, zt,
     xr, yr, zr, xl, yl, zl, exz, eyz, exy, ezy, eyx, ezx,
     hxm, hym, hzm,
-    placed_past, placed_new, placed_delay, proj,
-    part_old, part_new, recv_a_old, recv_a_new, sum_a_old, sum_a_new,
-    recv_b_old, recv_b_new, sum_b_old, sum_b_new, recv_c_old, recv_c_new,
+    placed_past, placed_new, placed_delay, proj, proj_one,
+    part_old, part_mid, part_new, recv_a_old, recv_a_mid, recv_a_new, sum_a_old, sum_a_mid, sum_a_new,
+    recv_b_old, recv_b_mid, recv_b_new, sum_b_old, sum_b_mid, sum_b_new,
+    out_c_old, out_c_mid, out_c_new, recv_c_old, recv_c_mid, recv_c_new,
     hs_sem, hr_sem, a_send, a_recv, b_send, b_recv, c_send, c_recv, in_sem,
 ):
-    n_x, n_y, n_z, sx, sy, sz, tiles, hpast, cap, old_rows, new_rows, share = dims
+    n_x, n_y, n_z, sx, sy, sz, tiles, hpast, cap, share = dims
     gx, gy, gz = lax.axis_index("gx"), lax.axis_index("gy"), lax.axis_index("gz")
     core, plane_z = gz % 2, gz // 2
     plane_n = n_y * (n_z // 2)
@@ -51,7 +52,7 @@
     for load in loads:
         load.start()
 
-    for ref in (xr, yr, zr, xl, yl, zl, exz, eyz, exy, ezy, eyx, ezx):
+    for ref in (xr, yr, zr, xl, yl, zl, exz, eyz, exy, ezy, eyx, ezx, out_c_old, out_c_mid, out_c_new):
         ref[...] = jnp.zeros_like(ref)
 
     barrier = pltpu.get_barrier_semaphore()
@@ -269,55 +270,100 @@
     loads[5].wait()
     loads[6].wait()
 
-    def project(source, time0, times, part, pad_rows, add, parity, first, count):
-        per = share // WIDE
-
-        def body(i, carry):
+    low_half = lax.broadcasted_iota(jnp.int32, (8, 128), 0) < 4
+    zero = jnp.zeros((8, 128), jnp.float32)
+
+    def shift_add(held, buf, times, base, column, piece, block, total):
+        for g in range(groups):
+            spot = g * wide_rows + block * 8
+            late = placed_delay[spot : spot + 8, pl.ds(column, 128)]
+            far_late = late > 1.5
+            odd = jnp.where(far_late, late - 2.0, late) > 0.5
+            value, once = None, [None, None]
+            for b in range(times + LAG - 1):
+                before, value = value, None
+                if b < times:
+                    at = b * slots + spot
+                    value = held[buf, at : at + 8, piece * 128 : piece * 128 + 128]
+                one = None
+                if value is not None or before is not None:
+                    one = jnp.where(odd, zero if before is None else before, zero if value is None else value)
+                two = once[0]
+                once = [once[1], one]
+                moved = jnp.where(far_late, zero if two is None else two, zero if one is None else one)
+                total[base + b] = moved if total[base + b] is None else total[base + b] + moved
+
+    def keep(part, member, inside, block, total, add):
+        def put(first, value):
+            spot = slice(first, first + value.shape[0])
+            if add:
+                value = part[member, inside, spot, :] + value
+            part[member, inside, spot, :] = value
+
+        if n_x == 4:
+            for b in range(0, len(total), 2):
+                pair = total[b : b + 2]
+                if add and all(v is None for v in pair):
+                    continue
+                first, second = [zero if v is None else v for v in pair]
+                across = jnp.where(low_half, second, first)
+                put(b * n_x, jnp.where(low_half, first, second) + pltpu.roll(across, 4, 0))
+            return
+        for b, value in enumerate(total):
+            if value is None:
+                if add:
+                    continue
+                value = zero
+            if n_x < 8:
+                whole = value
+                value = whole[0:n_x]
+                for other in range(n_x, 8, n_x):
+                    value = value + whole[other : other + n_x]
+            put(b * n_x + block * 8, value)
+
+    def project(source, time0, times, base, which, add, parity, held, wide):
+        part = sets[which][0]
+        bins = part.shape[2] // n_x
+        per = share // wide
+        count = plane_n * per
+
+        def multiply(i, buf):
             member = 2 * (i // per) + parity
-            start = pl.multiple_of(member * share + (i % per) * WIDE, WIDE)
-            proj[0 : times * slots, :] = jnp.dot(
-                source[time0 * slots : (time0 + times) * slots, :], weights_ref[:, pl.ds(start, WIDE)],
+            start = pl.multiple_of(member * share + (i % per) * wide, wide)
+            held[buf, 0 : times * slots, :] = jnp.dot(
+                source[time0 * slots : (time0 + times) * slots, :], weights_ref[:, pl.ds(start, wide)],
                 preferred_element_type=jnp.float32,
             )
-            for q in range(WIDE // 128):
-                column = pl.multiple_of(start + q * 128, 128)
-                inside = (i % per) * (WIDE // 128) + q
+
+        def gather(i, buf):
+            member = 2 * (i // per) + parity
+            for q in range(wide // 128):
+                inside = (i % per) * (wide // 128) + q
+                column = pl.multiple_of(member * share + inside * 128, 128)
                 for block in range(wide_rows // 8):
-                    bins = [None] * (time0 + times + LAG - 1)
-                    for g in range(groups):
-                        base = g * wide_rows + block * 8
-                        late = placed_delay[base : base + 8, pl.ds(column, 128)]
-                        keeps = [late == float(lag) for lag in range(LAG)]
-                        for t in range(times):
-                            value = proj[t * slots + base : t * slots + base + 8, q * 128 : q * 128 + 128]
-                            for lag in range(LAG):
-                                piece = jnp.where(keeps[lag], value, 0.0)
-                                b = time0 + t + lag
-                                bins[b] = piece if bins[b] is None else bins[b] + piece
-                    bins = bins + [None] * (pad_rows - len(bins))
-                    for b in range(pad_rows):
-                        if bins[b] is None:
-                            if add:
-                                continue
-                            bins[b] = jnp.zeros((8, 128), jnp.float32)
-                        if n_x >= 8:
-                            kept, many = bins[b], 8
-                        else:
-                            kept, many = bins[b][0:n_x], n_x
-                            for other in range(n_x, 8, n_x):
-                                kept = kept + bins[b][other : other + n_x]
-                        spot = pl.ds(block * 8 * pad_rows + b, many, stride=pad_rows)
-                        if add:
-                            kept = kept + part[member, inside, spot, :]
-                        part[member, inside, spot, :] = kept
+                    total = [None] * bins
+                    shift_add(held, buf, times, base, column, q, block, total)
+                    keep(part, member, inside, block, total, add)
+
+        def body(k, carry):
+            multiply(2 * k + 1, 1)
+            gather(2 * k, 0)
+            multiply(2 * k + 2, 0)
+            gather(2 * k + 1, 1)
             return carry
 
-        lax.fori_loop(first, first + count, body, 0)
+        multiply(0, 0)
+        lax.fori_loop(0, count // 2 - 1, body, 0)
+        multiply(count - 1, 1)
+        gather(count - 2, 0)
+        gather(count - 1, 1)
 
     sets = (
-        (part_old, recv_a_old, sum_a_old, recv_b_old, sum_b_old, recv_c_old, old_rows),
-        (part_new, recv_a_new, sum_a_new, recv_b_new, sum_b_new, recv_c_new, new_rows),
-    )
+        (part_old, recv_a_old, sum_a_old, recv_b_old, sum_b_old, out_c_old, recv_c_old),
+        (part_mid, recv_a_mid, sum_a_mid, recv_b_mid, sum_b_mid, out_c_mid, recv_c_mid),
+        (part_new, recv_a_new, sum_a_new, recv_b_new, sum_b_new, out_c_new, recv_c_new),
+    )
+    kept_bins = (hpast + LAG - 1, STEPS - 1 + LAG - 1, LAG)
 
     def copy_a(which, m):
         part, recv = sets[which][0], sets[which][1]
@@ -329,7 +375,8 @@
         )
 
     blocks = share // 128
-    cuts = ((0, blocks // 2, blocks), (0, blocks))
+    cuts = ((0, blocks // 2, blocks), (0, blocks), (0, blocks))
+    b_base = (0, 2, 3)
 
     def copy_b(which, piece, j):
         span = slice(cuts[which][piece], cuts[which][piece + 1])
@@ -338,15 +385,15 @@
         half = n_z // 2
         return pltpu.make_async_remote_copy(
             src_ref=summed.at[other, span], dst_ref=recv.at[j, span],
-            send_sem=b_send.at[2 * which + piece, j], recv_sem=b_recv.at[2 * which + piece, j],
+            send_sem=b_send.at[b_base[which] + piece, j], recv_sem=b_recv.at[b_base[which] + piece, j],
             device_id=(gx, other // half, (other % half) * 2 + core), device_id_type=MESH,
         )
 
     def copy_c(which, j):
-        summed, recv, rows = sets[which][4], sets[which][5], sets[which][6]
+        source, recv = sets[which][5], sets[which][6]
         other = (gx + j) % n_x
         return pltpu.make_async_remote_copy(
-            src_ref=summed.at[:, pl.ds(pl.multiple_of(other * rows, 8), rows)], dst_ref=recv.at[j],
+            src_ref=source.at[other], dst_ref=recv.at[j],
             send_sem=c_send.at[which, j], recv_sem=c_recv.at[which, j],
             device_id=(other, gy, gz), device_id_type=MESH,
         )
@@ -370,16 +417,20 @@
             for piece in range(len(cuts[which]) - 1):
                 copy_b(which, piece, j).wait_recv()
             total = total + sets[which][3][j]
-        sets[which][4][...] = total
+        summed, source = sets[which][4], sets[which][5]
+        summed[...] = total
+        many = kept_bins[which]
+        for s in range(n_x):
+            for q in range(blocks):
+                source[s, q, 0:many, :] = summed[q, pl.ds(s, many, stride=n_x), :]
         for j in range(1, n_x):
             copy_c(which, j).start()
 
     def end_c(which):
-        rows = sets[which][6]
-        total = sets[which][4][:, pl.ds(pl.multiple_of(gx * rows, 8), rows), :]
+        total = sets[which][5][gx]
         for j in range(1, n_x):
             copy_c(which, j).wait_recv()
-            total = total + sets[which][5][j]
+            total = total + sets[which][6][j]
         for m in range(plane_n):
             copy_a(which, m).wait_send()
         for j in range(1, plane_n):
@@ -389,7 +440,6 @@
             copy_c(which, j).wait_send()
         return total
 
-    chunks = plane_n * share // WIDE
     other = 1 - core
 
     def sample(step):
@@ -399,28 +449,34 @@
                 sampler, flat, preferred_element_type=jnp.float32
             ).astype(jnp.bfloat16)
 
-    def past(parity, first, count):
-        project(placed_past, 0, hpast, part_old, old_rows, False, parity, first, count)
-
-    def early(parity, first, count):
-        project(placed_new, 0, STEPS - 1, part_new, new_rows, False, parity, first, count)
-
-    def last(parity):
-        project(placed_new, STEPS - 1, 1, part_new, new_rows, True, parity, 0, chunks)
+    def past(parity):
+        project(placed_past, 0, hpast, 0, 0, False, parity, proj, WIDE)
+
+    def recent(parity, step):
+        if step < STEPS - 1:
+            project(placed_new, step, 1, step, 1, step > 0, parity, proj_one, share)
+        else:
+            project(placed_new, step, 1, 0, 2, False, parity, proj_one, share)
 
     def beside(step):
         if step == 0:
-            past(other, 0, chunks)
+            past(other)
             begin_a(0)
-            past(core, 0, chunks)
+            past(core)
         elif step == 1:
             a_to_b(0)
+            recent(other, 0)
+            recent(core, 0)
         elif step == 2:
             for j in range(1, plane_n):
                 copy_b(0, 1, j).start()
+            recent(other, 1)
+            recent(core, 1)
         elif step == 3:
-            early(other, 0, chunks)
-            early(core, 0, chunks)
+            recent(other, 2)
+            begin_a(1)
+            recent(core, 2)
+            a_to_b(1)
             b_to_c(0)
 
     for step in range(STEPS):
@@ -435,26 +491,29 @@
             sample(step)
         else:
             sample(step)
-            last(other)
-            begin_a(1)
-            last(core)
+            recent(other, step)
+            begin_a(2)
+            recent(core, step)
+            a_to_b(2)
             update_below(step, False)
             update_e(step)
-    a_to_b(1)
     scale = float(tiles * members) ** (-0.5)
-    old = end_c(0)
     for step in range(STEPS):
         end_halo(step)
     b_to_c(1)
+    old = end_c(0)
     far_ref[...] = jnp.zeros_like(far_ref)
-    new = end_c(1)
-    used = min(new_rows, NB - hpast)
-    for q in range(share // 128):
-        columns = slice(q * 128, q * 128 + 128)
-        far_ref[0:old_rows, columns] = old[q] * scale
-        far_ref[hpast : hpast + used, columns] = (
-            far_ref[hpast : hpast + used, columns] + (new[q] * scale)[0:used]
-        )
+    for q in range(blocks):
+        far_ref[0 : kept_bins[0], q * 128 : q * 128 + 128] = (old[q] * scale)[0 : kept_bins[0]]
+    b_to_c(2)
+    for which, first in ((1, hpast), (2, hpast + STEPS - 1)):
+        many = kept_bins[which]
+        total = end_c(which)
+        for q in range(blocks):
+            columns = slice(q * 128, q * 128 + 128)
+            far_ref[first : first + many, columns] = (
+                far_ref[first : first + many, columns] + (total[q] * scale)[0:many]
+            )
 
 
 def store_kernel(e_ref, far_ref, eout_ref, fout_ref, sem):
@@ -482,8 +541,8 @@
     plane_n = n_y * (n_z // 2)
     directions = weights.shape[1]
     share = directions // members
-    old_rows, new_rows = up8(hpast + LAG - 1), up8(STEPS + LAG - 1)
-    dims = (n_x, n_y, n_z, sx, sy, sz, tiles, hpast, cap, old_rows, new_rows, share)
+    dims = (n_x, n_y, n_z, sx, sy, sz, tiles, hpast, cap, share)
+    kept_bins = (hpast + LAG - 1, STEPS - 1 + LAG - 1, LAG)
     anywhere, resident = pl.BlockSpec(memory_space=pl.ANY), pl.BlockSpec(memory_space=pltpu.VMEM)
     f32, bf16 = jnp.float32, jnp.bfloat16
     vmem = pltpu.VMEM
@@ -493,7 +552,7 @@
     flat, rows8 = vmem((STEPS, sy, sz), f32), vmem((STEPS, 8, sz), f32)
     edges = [flat, rows8] + [vmem((STEPS, 2, sx, sz), f32)] * 2 + [rows8, flat]
     below = [vmem((2, sy, sz), f32), vmem((2, sx, sz), f32), vmem((2, sy, sz), f32)]
-    per_set = lambda make: [make(n_x * old_rows, old_rows), make(n_x * new_rows, new_rows)]
+    per_set = lambda make: [make(up8(n_x * bins), up8(bins)) for bins in kept_bins]
     scratch = (
         [vmem((3, sx, sy, sz), f32), vmem((sx, sy, sz), f32)]
         + [vmem((hpast, tiles, width), bf16), vmem((1, tiles), jnp.int32), vmem((1, tiles), jnp.int32)]
@@ -508,7 +567,8 @@
             vmem((hpast * slots, width), bf16),
             vmem((STEPS * slots, width), bf16),
             vmem((slots, directions), f32),
-            vmem((max(hpast, STEPS) * slots, WIDE), f32),
+            vmem((2, hpast * slots, WIDE), f32),
+            vmem((2, slots, share), f32),
         ]
         + per_set(lambda rows, one: vmem((members, share // 128, rows, 128), f32))
         + per_set(lambda rows, one: vmem((plane_n, share // 128, rows, 128), f32))
@@ -516,10 +576,11 @@
         + per_set(lambda rows, one: vmem((plane_n, share // 128, rows, 128), f32))
         + per_set(lambda rows, one: vmem((share // 128, rows, 128), f32))
         + per_set(lambda rows, one: vmem((n_x, share // 128, one, 128), f32))
+        + per_set(lambda rows, one: vmem((n_x, share // 128, one, 128), f32))
         + [pltpu.SemaphoreType.DMA((STEPS, 12))] * 2
-        + [pltpu.SemaphoreType.DMA((2, plane_n))] * 2
         + [pltpu.SemaphoreType.DMA((3, plane_n))] * 2
-        + [pltpu.SemaphoreType.DMA((2, n_x))] * 2
+        + [pltpu.SemaphoreType.DMA((4, plane_n))] * 2
+        + [pltpu.SemaphoreType.DMA((3, n_x))] * 2
         + [pltpu.SemaphoreType.DMA((7,))]
     )
     efield, far = pl.pallas_call(

time: 40.1 us -> 35.1 us (0.88)
  Pallas kernels: 39.3 us -> 34.3 us
    pallas_call x1, Pallas kernels: 38.4 us -> 33.3 us  [local(): pl.pallas_call(functools.partial(kernel, dims), out_shape=(vmem(initial_f...]
where the time goes in v2:
time: 35.1 us; the launch traced here: 34.9 us
  Pallas kernels  34.3 us (98%)
  between operations  0.64 us (2%)
    pallas_call x1, Pallas kernels, local(): pl.pallas_call(functools.partial(kernel, dims), out_shape=(vmem(initial_f...  33.3 us
    pallas_call x1, Pallas kernels, local(): pl.pallas_call(store_kernel, out_shape=(jax.ShapeDtypeStruct(initial_fiel...  0.97 us

profile of v2, /device:TPU:0, one launch (start us, length us, event | category | flops | bytes accessed | tf_op | source)
XLA Modules:
  0.0 34.9 jit_solution(2589099992891647298)
XLA Ops:
  0.6 33.3 %shard_map.86 = (f32[3,8,32,128]{3,2,1,0:T(8,128)S(1)}, f32[20,512]{1,0:T(8,128)S(1)}) custom-call(f32[3,8,32,128]{3,2,1,0:T(8,128)} %field_ref.1, f32[8,32,128]{2,1,0:T(8,128)} %perm_ref.1, bf16[12,24,256]{2,1,0:T(8,128)(2,1)} %bitcast.4, s32[1,24]{1,0:T(1,128)} %bitcast.5, s32[1,24]{1,0:T(1,128)} %bitcast.6, s32[24,4096]{1,0:T(8,128)} %delays_hbm.1, ...), custom_call_target="tpu_custom_call" | custom-call | tf_op jit(solution)/shard_map/pallas_call | solution.py:586
  33.9 1.0 %shard_map.87 = (f32[3,8,32,128]{3,2,1,0:T(8,128)}, f32[20,1,512]{2,1,0:T(1,128)}) custom-call(f32[3,8,32,128]{3,2,1,0:T(8,128)S(1)} %get-tuple-element.6.e_ref, f32[20,512]{1,0:T(8,128)S(1)} %get-tuple-element.7.far_ref), custom_call_target="tpu_custom_call" | custom-call | tf_op jit(solution)/shard_map/pallas_call | solution.py:601

commit v3 on v2

--- a/solution.py
+++ b/solution.py
@@ -13,7 +13,6 @@
 
 courant = 0.5
 MESH = pl.DeviceIdType.MESH
-WIDE = 256
 
 
 def kernel(
@@ -21,7 +20,7 @@
     field_ref, perm_ref, hist_hbm, rows_hbm, owners_hbm, delays_hbm, weights_hbm,
     e, far_ref,
     h, perm, hist_ref, rows_ref, owners_ref, delays_ref, weights_ref,
-    xs, ys, zs, xt, yt, zt,
+    xs, ys, zs, xt, yt, zt, cx, cz,
     xr, yr, zr, xl, yl, zl, exz, eyz, exy, ezy, eyx, ezx,
     hxm, hym, hzm,
     placed_past, placed_new, placed_delay, proj, proj_one,
@@ -67,14 +66,14 @@
 
     tail = slice(sy - 8, sy)
     copies = (
+        ((1, 0, -1), lambda k: cz.at[k], lambda k: exz.at[k]),
+        ((-1, 0, 1), lambda k: cx.at[k], lambda k: ezx.at[k]),
+        ((1, -1, 0), lambda k: ys.at[k, 0], lambda k: exy.at[k]),
+        ((-1, 1, 0), lambda k: xs.at[k, 0, tail], lambda k: eyx.at[k]),
+        ((1, 0, 0), lambda k: xt.at[k], lambda k: xl.at[k]),
         ((-1, 0, 0), lambda k: xs.at[k], lambda k: xr.at[k]),
-        ((1, 0, 0), lambda k: xt.at[k], lambda k: xl.at[k]),
-        ((1, 0, -1), lambda k: zs.at[k], lambda k: exz.at[k]),
-        ((-1, 0, 1), lambda k: xs.at[k, 1], lambda k: ezx.at[k]),
-        ((1, -1, 0), lambda k: ys.at[k], lambda k: exy.at[k]),
-        ((-1, 1, 0), lambda k: xs.at[k, 0, tail], lambda k: eyx.at[k]),
         ((0, 1, -1), lambda k: zs.at[k, tail], lambda k: eyz.at[k]),
-        ((0, -1, 1), lambda k: ys.at[k], lambda k: ezy.at[k]),
+        ((0, -1, 1), lambda k: ys.at[k, 1], lambda k: ezy.at[k]),
         ((0, -1, 0), lambda k: ys.at[k], lambda k: yr.at[k]),
         ((0, 1, 0), lambda k: yt.at[k], lambda k: yl.at[k]),
         ((0, 0, -1), lambda k: zs.at[k], lambda k: zr.at[k]),
@@ -99,11 +98,27 @@
     lane = lax.broadcasted_iota(jnp.int32, (sy, sz), 1)
     row = lax.broadcasted_iota(jnp.int32, (sy, sz), 0)
 
+    lane_row = lax.broadcasted_iota(jnp.int32, (8, sz), 1)
+
+    def pack_column(v, at):
+        tile = jnp.zeros((8, sz), jnp.float32)
+        for j in range(sy // 8):
+            tile = jnp.where(lane_row == j, pltpu.roll(v[8 * j : 8 * j + 8], (j - at) % sz, 1), tile)
+        return tile
+
+    def spread_column(tile, at):
+        return jnp.concatenate([pltpu.roll(tile, (at - j) % sz, 1) for j in range(sy // 8)], axis=0)
+
     def stage(slot):
         for i, c in enumerate((1, 2)):
             xs[slot, i] = e[c, 0]
-        for c in range(3):
-            xt[slot, c] = e[c, sx - 1]
+        ex, ey, ez = e[0, sx - 1], e[1, sx - 1], e[2, sx - 1]
+        ex_z = jnp.where(lane == sz - 1, 0.0, pltpu.roll(ex, sz - 1, 1))
+        ex_y = jnp.where(row == sy - 1, 0.0, pltpu.roll(ex, sy - 1, 0))
+        xt[slot, 0] = (ex_z - ex) + ez
+        xt[slot, 1] = (ex - ex_y) - ey
+        cz[slot] = pack_column(ex, 0)
+        cx[slot] = pack_column(e[2, 0], sz - 1)
         for i, c in enumerate((0, 2)):
             for x in range(sx):
                 ys[slot, i, x : x + 1, :] = e[c, x, 0:1, :]
@@ -175,13 +190,10 @@
             fresh = -change if first else ref[i] - change
             ref[i] = jnp.where(exists, fresh, 0.0)
 
-        ex, ey, ez = xl[slot, 0], xl[slot, 1], xl[slot, 2]
-        ex_z = jnp.where(
-            lane == sz - 1, pltpu.roll(exz[slot], sz - sx, 1), pltpu.roll(ex, sz - 1, 1)
-        )
-        ex_y = jnp.where(row == sy - 1, exy[slot, 0, sx - 1 : sx, :], pltpu.roll(ex, sy - 1, 0))
-        put(hxm, 0, courant * ((ex_z - ex) - (xs[slot, 1] - ez)), gx > 0)
-        put(hxm, 1, courant * ((xs[slot, 0] - ey) - (ex_y - ex)), gx > 0)
+        ex_z = jnp.where(lane == sz - 1, spread_column(exz[slot], sz - 1), 0.0)
+        ex_y = jnp.where(row == sy - 1, exy[slot, sx - 1 : sx, :], 0.0)
+        put(hxm, 0, courant * ((xl[slot, 0] + ex_z) - xs[slot, 1]), gx > 0)
+        put(hxm, 1, courant * ((xl[slot, 1] - ex_y) + xs[slot, 0]), gx > 0)
 
         ex, ey, ez = yl[slot, 0], yl[slot, 1], yl[slot, 2]
         edge = jnp.sum(
@@ -198,10 +210,10 @@
         ez = pltpu.roll(ex, sz - 2 * sx, 1)
         ex_up = zs[slot]
         ey_up = pltpu.roll(ex_up, sz - sx, 1)
-        column = jnp.sum(jnp.where(lane8 == sz - 1, ezy[slot, 1], 0.0), axis=1, keepdims=True)
+        column = jnp.sum(jnp.where(lane8 == sz - 1, ezy[slot], 0.0), axis=1, keepdims=True)
         edge = jnp.sum(jnp.where(lane8 == row8, column, 0.0), axis=0, keepdims=True)
         ez_y = jnp.where(row == sy - 1, edge, pltpu.roll(ez, sy - 1, 0))
-        ez_x = jnp.where(lane == sx - 1, pltpu.roll(ezx[slot], sx, 1), pltpu.roll(ez, sz - 1, 1))
+        ez_x = jnp.where(lane == sx - 1, spread_column(ezx[slot], sx - 1), pltpu.roll(ez, sz - 1, 1))
         put(hzm, 0, courant * ((ez_y - ez) - (ey_up - ey)), gz > 0)
         put(hzm, 1, courant * ((ex_up - ex) - (ez_x - ez)), gz > 0)
 
@@ -321,24 +333,21 @@
                     value = value + whole[other : other + n_x]
             put(b * n_x + block * 8, value)
 
-    def project(source, time0, times, base, which, add, parity, held, wide):
+    def project(source, time0, times, base, which, add, parity, held, wide, half):
         part = sets[which][0]
         bins = part.shape[2] // n_x
-        per = share // wide
-        count = plane_n * per
-
-        def multiply(i, buf):
-            member = 2 * (i // per) + parity
-            start = pl.multiple_of(member * share + (i % per) * wide, wide)
+
+        def multiply(m, buf):
+            start = pl.multiple_of((2 * m + parity) * share + half * wide, 128)
             held[buf, 0 : times * slots, :] = jnp.dot(
                 source[time0 * slots : (time0 + times) * slots, :], weights_ref[:, pl.ds(start, wide)],
                 preferred_element_type=jnp.float32,
             )
 
-        def gather(i, buf):
-            member = 2 * (i // per) + parity
+        def gather(m, buf):
+            member = 2 * m + parity
             for q in range(wide // 128):
-                inside = (i % per) * (wide // 128) + q
+                inside = half * (wide // 128) + q
                 column = pl.multiple_of(member * share + inside * 128, 128)
                 for block in range(wide_rows // 8):
                     total = [None] * bins
@@ -353,10 +362,10 @@
             return carry
 
         multiply(0, 0)
-        lax.fori_loop(0, count // 2 - 1, body, 0)
-        multiply(count - 1, 1)
-        gather(count - 2, 0)
-        gather(count - 1, 1)
+        lax.fori_loop(0, plane_n // 2 - 1, body, 0)
+        multiply(plane_n - 1, 1)
+        gather(plane_n - 2, 0)
+        gather(plane_n - 1, 1)
 
     sets = (
         (part_old, recv_a_old, sum_a_old, recv_b_old, sum_b_old, out_c_old, recv_c_old),
@@ -365,18 +374,19 @@
     )
     kept_bins = (hpast + LAG - 1, STEPS - 1 + LAG - 1, LAG)
 
-    def copy_a(which, m):
+    blocks = share // 128
+    cuts = ((0, blocks // 2, blocks), (0, blocks), (0, blocks))
+    sem_base = (0, 2, 3)
+
+    def copy_a(which, piece, m):
+        span = slice(cuts[which][piece], cuts[which][piece + 1])
         part, recv = sets[which][0], sets[which][1]
         other = 1 - core
         return pltpu.make_async_remote_copy(
-            src_ref=part.at[2 * m + other], dst_ref=recv.at[m],
-            send_sem=a_send.at[which, m], recv_sem=a_recv.at[which, m],
+            src_ref=part.at[2 * m + other, span], dst_ref=recv.at[m, span],
+            send_sem=a_send.at[sem_base[which] + piece, m], recv_sem=a_recv.at[sem_base[which] + piece, m],
             device_id=(gx, gy, plane_z * 2 + other), device_id_type=MESH,
         )
-
-    blocks = share // 128
-    cuts = ((0, blocks // 2, blocks), (0, blocks), (0, blocks))
-    b_base = (0, 2, 3)
 
     def copy_b(which, piece, j):
         span = slice(cuts[which][piece], cuts[which][piece + 1])
@@ -385,7 +395,7 @@
         half = n_z // 2
         return pltpu.make_async_remote_copy(
             src_ref=summed.at[other, span], dst_ref=recv.at[j, span],
-            send_sem=b_send.at[b_base[which] + piece, j], recv_sem=b_recv.at[b_base[which] + piece, j],
+            send_sem=b_send.at[sem_base[which] + piece, j], recv_sem=b_recv.at[sem_base[which] + piece, j],
             device_id=(gx, other // half, (other % half) * 2 + core), device_id_type=MESH,
         )
 
@@ -398,18 +408,19 @@
             device_id=(other, gy, gz), device_id_type=MESH,
         )
 
-    def begin_a(which):
+    def begin_a(which, piece):
         for m in range(plane_n):
-            copy_a(which, m).start()
-
-    def a_to_b(which):
+            copy_a(which, piece, m).start()
+
+    def a_to_b(which, piece):
+        span = slice(cuts[which][piece], cuts[which][piece + 1])
         part, recv, summed = sets[which][0], sets[which][1], sets[which][2]
         for j in list(range(1, plane_n)) + [0]:
             m = (plane_me + j) % plane_n
-            copy_a(which, m).wait_recv()
-            summed[m] = part[2 * m + core] + recv[m]
+            copy_a(which, piece, m).wait_recv()
+            summed[m, span] = part[2 * m + core, span] + recv[m, span]
             if j > 0:
-                copy_b(which, 0, j).start()
+                copy_b(which, piece, j).start()
 
     def b_to_c(which):
         total = sets[which][2][plane_me]
@@ -432,7 +443,8 @@
             copy_c(which, j).wait_recv()
             total = total + sets[which][6][j]
         for m in range(plane_n):
-            copy_a(which, m).wait_send()
+            for piece in range(len(cuts[which]) - 1):
+                copy_a(which, piece, m).wait_send()
         for j in range(1, plane_n):
             for piece in range(len(cuts[which]) - 1):
                 copy_b(which, piece, j).wait_send()
@@ -449,35 +461,34 @@
                 sampler, flat, preferred_element_type=jnp.float32
             ).astype(jnp.bfloat16)
 
-    def past(parity):
-        project(placed_past, 0, hpast, 0, 0, False, parity, proj, WIDE)
-
-    def recent(parity, step):
-        if step < STEPS - 1:
-            project(placed_new, step, 1, step, 1, step > 0, parity, proj_one, share)
-        else:
-            project(placed_new, step, 1, 0, 2, False, parity, proj_one, share)
+    def past(half):
+        for parity in (other, core):
+            project(placed_past, 0, hpast, 0, 0, False, parity, proj, share // 2, half)
+            if parity is other:
+                begin_a(0, half)
+
+    def recent(step):
+        which = 1 if step < STEPS - 1 else 2
+        base = step if step < STEPS - 1 else 0
+        for parity in (other, core):
+            project(placed_new, step, 1, base, which, 0 < step < STEPS - 1, parity, proj_one, share, 0)
+            if parity is other and step >= STEPS - 2:
+                begin_a(which, 0)
 
     def beside(step):
         if step == 0:
-            past(other)
-            begin_a(0)
-            past(core)
+            past(0)
         elif step == 1:
-            a_to_b(0)
-            recent(other, 0)
-            recent(core, 0)
+            a_to_b(0, 0)
+            past(1)
+            recent(0)
         elif step == 2:
-            for j in range(1, plane_n):
-                copy_b(0, 1, j).start()
-            recent(other, 1)
-            recent(core, 1)
+            a_to_b(0, 1)
+            recent(1)
         elif step == 3:
-            recent(other, 2)
-            begin_a(1)
-            recent(core, 2)
-            a_to_b(1)
+            recent(2)
             b_to_c(0)
+            a_to_b(1, 0)
 
     for step in range(STEPS):
         beside(step)
@@ -491,10 +502,8 @@
             sample(step)
         else:
             sample(step)
-            recent(other, step)
-            begin_a(2)
-            recent(core, step)
-            a_to_b(2)
+            recent(step)
+            a_to_b(2, 0)
             update_below(step, False)
             update_e(step)
     scale = float(tiles * members) ** (-0.5)
@@ -546,28 +555,29 @@
     anywhere, resident = pl.BlockSpec(memory_space=pl.ANY), pl.BlockSpec(memory_space=pltpu.VMEM)
     f32, bf16 = jnp.float32, jnp.bfloat16
     vmem = pltpu.VMEM
-    faces = lambda low: [
-        vmem((STEPS, low, sy, sz), f32), vmem((STEPS, low, sx, sz), f32), vmem((STEPS, sy, sz), f32)
+    faces = lambda in_x, in_y: [
+        vmem((STEPS, in_x, sy, sz), f32), vmem((STEPS, in_y, sx, sz), f32), vmem((STEPS, sy, sz), f32)
     ]
-    flat, rows8 = vmem((STEPS, sy, sz), f32), vmem((STEPS, 8, sz), f32)
-    edges = [flat, rows8] + [vmem((STEPS, 2, sx, sz), f32)] * 2 + [rows8, flat]
+    rows8 = vmem((STEPS, 8, sz), f32)
+    edges = [rows8, rows8] + [vmem((STEPS, sx, sz), f32)] * 2 + [rows8, rows8]
     below = [vmem((2, sy, sz), f32), vmem((2, sx, sz), f32), vmem((2, sy, sz), f32)]
     per_set = lambda make: [make(up8(n_x * bins), up8(bins)) for bins in kept_bins]
     scratch = (
         [vmem((3, sx, sy, sz), f32), vmem((sx, sy, sz), f32)]
         + [vmem((hpast, tiles, width), bf16), vmem((1, tiles), jnp.int32), vmem((1, tiles), jnp.int32)]
         + [vmem(delays.shape, jnp.int32), vmem(weights.shape, bf16)]
-        + faces(2)
-        + faces(3)
-        + faces(2)
-        + faces(3)
+        + faces(2, 2)
+        + faces(2, 3)
+        + [rows8, rows8]
+        + faces(2, 2)
+        + faces(2, 3)
         + edges
         + below
         + [
             vmem((hpast * slots, width), bf16),
             vmem((STEPS * slots, width), bf16),
             vmem((slots, directions), f32),
-            vmem((2, hpast * slots, WIDE), f32),
+            vmem((2, hpast * slots, share // 2), f32),
             vmem((2, slots, share), f32),
         ]
         + per_set(lambda rows, one: vmem((members, share // 128, rows, 128), f32))
@@ -578,8 +588,7 @@
         + per_set(lambda rows, one: vmem((n_x, share // 128, one, 128), f32))
         + per_set(lambda rows, one: vmem((n_x, share // 128, one, 128), f32))
         + [pltpu.SemaphoreType.DMA((STEPS, 12))] * 2
-        + [pltpu.SemaphoreType.DMA((3, plane_n))] * 2
-        + [pltpu.SemaphoreType.DMA((4, plane_n))] * 2
+        + [pltpu.SemaphoreType.DMA((4, plane_n))] * 4
         + [pltpu.SemaphoreType.DMA((3, n_x))] * 2
         + [pltpu.SemaphoreType.DMA((7,))]
     )

time: 35.1 us -> 33.1 us (0.943)
  Pallas kernels: 34.3 us -> 32.3 us
    pallas_call x1, Pallas kernels: 33.3 us -> 31.3 us  [local(): pl.pallas_call(functools.partial(kernel, dims), out_shape=(vmem(initial_f...]
where the time goes in v3:
time: 33.1 us; the launch traced here: 32.9 us
  Pallas kernels  32.3 us (98%)
  between operations  0.64 us (2%)
    pallas_call x1, Pallas kernels, local(): pl.pallas_call(functools.partial(kernel, dims), out_shape=(vmem(initial_f...  31.3 us
    pallas_call x1, Pallas kernels, local(): pl.pallas_call(store_kernel, out_shape=(jax.ShapeDtypeStruct(initial_fiel...  0.97 us

profile of v3, /device:TPU:0, one launch (start us, length us, event | category | flops | bytes accessed | tf_op | source)
XLA Modules:
  0.0 32.9 jit_solution(9791173892044827633)
XLA Ops:
  0.6 31.3 %shard_map.86 = (f32[3,8,32,128]{3,2,1,0:T(8,128)S(1)}, f32[20,512]{1,0:T(8,128)S(1)}) custom-call(f32[3,8,32,128]{3,2,1,0:T(8,128)} %field_ref.1, f32[8,32,128]{2,1,0:T(8,128)} %perm_ref.1, bf16[12,24,256]{2,1,0:T(8,128)(2,1)} %bitcast.4, s32[1,24]{1,0:T(1,128)} %bitcast.5, s32[1,24]{1,0:T(1,128)} %bitcast.6, s32[24,4096]{1,0:T(8,128)} %delays_hbm.1, ...), custom_call_target="tpu_custom_call" | custom-call | tf_op jit(solution)/shard_map/pallas_call | solution.py:595
  31.9 1.0 %shard_map.87 = (f32[3,8,32,128]{3,2,1,0:T(8,128)}, f32[20,1,512]{2,1,0:T(1,128)}) custom-call(f32[3,8,32,128]{3,2,1,0:T(8,128)S(1)} %get-tuple-element.6.e_ref, f32[20,512]{1,0:T(8,128)S(1)} %get-tuple-element.7.far_ref), custom_call_target="tpu_custom_call" | custom-call | tf_op jit(solution)/shard_map/pallas_call | solution.py:610

commit v4 on v3

--- a/solution.py
+++ b/solution.py
@@ -140,7 +140,7 @@
         offset, source, target = copies[number]
         return pltpu.make_async_remote_copy(
             src_ref=source(slot), dst_ref=target(slot),
-            send_sem=hs_sem.at[slot, number], recv_sem=hr_sem.at[slot, number],
+            send_sem=hs_sem.at[number], recv_sem=hr_sem.at[slot % 2, number],
             device_id=at_offset(offset, 1)[1], device_id_type=MESH,
         )
 
@@ -384,7 +384,7 @@
         other = 1 - core
         return pltpu.make_async_remote_copy(
             src_ref=part.at[2 * m + other, span], dst_ref=recv.at[m, span],
-            send_sem=a_send.at[sem_base[which] + piece, m], recv_sem=a_recv.at[sem_base[which] + piece, m],
+            send_sem=a_send.at[m], recv_sem=a_recv.at[(sem_base[which] + piece) % 2, m],
             device_id=(gx, gy, plane_z * 2 + other), device_id_type=MESH,
         )
 
@@ -395,7 +395,7 @@
         half = n_z // 2
         return pltpu.make_async_remote_copy(
             src_ref=summed.at[other, span], dst_ref=recv.at[j, span],
-            send_sem=b_send.at[sem_base[which] + piece, j], recv_sem=b_recv.at[sem_base[which] + piece, j],
+            send_sem=b_send.at[j - 1], recv_sem=b_recv.at[sem_base[which] + piece, j - 1],
             device_id=(gx, other // half, (other % half) * 2 + core), device_id_type=MESH,
         )
 
@@ -404,12 +404,21 @@
         other = (gx + j) % n_x
         return pltpu.make_async_remote_copy(
             src_ref=source.at[other], dst_ref=recv.at[j],
-            send_sem=c_send.at[which, j], recv_sem=c_recv.at[which, j],
+            send_sem=c_send.at[j - 1], recv_sem=c_recv.at[which, j - 1],
             device_id=(other, gy, gz), device_id_type=MESH,
         )
 
+    turns = ((0, 0), (0, 1), (1, 0), (2, 0))
+
+    def turn_before(which, piece):
+        at = turns.index((which, piece))
+        return turns[at - 1] if at > 0 else None
+
     def begin_a(which, piece):
+        before = turn_before(which, piece)
         for m in range(plane_n):
+            if before:
+                copy_a(*before, m).wait_send()
             copy_a(which, piece, m).start()
 
     def a_to_b(which, piece):
@@ -420,6 +429,8 @@
             copy_a(which, piece, m).wait_recv()
             summed[m, span] = part[2 * m + core, span] + recv[m, span]
             if j > 0:
+                if turn_before(which, piece):
+                    copy_b(*turn_before(which, piece), j).wait_send()
                 copy_b(which, piece, j).start()
 
     def b_to_c(which):
@@ -435,6 +446,8 @@
             for q in range(blocks):
                 source[s, q, 0:many, :] = summed[q, pl.ds(s, many, stride=n_x), :]
         for j in range(1, n_x):
+            if which > 0:
+                copy_c(which - 1, j).wait_send()
             copy_c(which, j).start()
 
     def end_c(which):
@@ -442,14 +455,13 @@
         for j in range(1, n_x):
             copy_c(which, j).wait_recv()
             total = total + sets[which][6][j]
-        for m in range(plane_n):
-            for piece in range(len(cuts[which]) - 1):
-                copy_a(which, piece, m).wait_send()
-        for j in range(1, plane_n):
-            for piece in range(len(cuts[which]) - 1):
-                copy_b(which, piece, j).wait_send()
-        for j in range(1, n_x):
-            copy_c(which, j).wait_send()
+        if which == 2:
+            for m in range(plane_n):
+                copy_a(which, 0, m).wait_send()
+            for j in range(1, plane_n):
+                copy_b(which, 0, j).wait_send()
+            for j in range(1, n_x):
+                copy_c(which, j).wait_send()
         return total
 
     other = 1 - core
@@ -498,6 +510,7 @@
             update_below(step, step == 0)
             update_e(step)
             stage(step + 1)
+            end_halo(step)
             send_halo(step + 1)
             sample(step)
         else:
@@ -507,8 +520,7 @@
             update_below(step, False)
             update_e(step)
     scale = float(tiles * members) ** (-0.5)
-    for step in range(STEPS):
-        end_halo(step)
+    end_halo(STEPS - 1)
     b_to_c(1)
     old = end_c(0)
     far_ref[...] = jnp.zeros_like(far_ref)
@@ -587,9 +599,10 @@
         + per_set(lambda rows, one: vmem((share // 128, rows, 128), f32))
         + per_set(lambda rows, one: vmem((n_x, share // 128, one, 128), f32))
         + per_set(lambda rows, one: vmem((n_x, share // 128, one, 128), f32))
-        + [pltpu.SemaphoreType.DMA((STEPS, 12))] * 2
-        + [pltpu.SemaphoreType.DMA((4, plane_n))] * 4
-        + [pltpu.SemaphoreType.DMA((3, n_x))] * 2
+        + [pltpu.SemaphoreType.DMA((12,)), pltpu.SemaphoreType.DMA((2, 12))]
+        + [pltpu.SemaphoreType.DMA((plane_n,)), pltpu.SemaphoreType.DMA((2, plane_n))]
+        + [pltpu.SemaphoreType.DMA((plane_n - 1,)), pltpu.SemaphoreType.DMA((4, plane_n - 1))]
+        + [pltpu.SemaphoreType.DMA((n_x - 1,)), pltpu.SemaphoreType.DMA((3, n_x - 1))]
         + [pltpu.SemaphoreType.DMA((7,))]
     )
     efield, far = pl.pallas_call(

time: 33.1 us -> 32.6 us (0.985)
  Pallas kernels: 32.3 us -> 31.8 us
    pallas_call x1, Pallas kernels: 31.3 us -> 30.8 us  [local(): pl.pallas_call(functools.partial(kernel, dims), out_shape=(vmem(initial_f...]
where the time goes in v4:
time: 32.6 us; the launch traced here: 32.4 us
  Pallas kernels  31.8 us (98%)
  between operations  0.64 us (2%)
    pallas_call x1, Pallas kernels, local(): pl.pallas_call(functools.partial(kernel, dims), out_shape=(vmem(initial_f...  30.8 us
    pallas_call x1, Pallas kernels, local(): pl.pallas_call(store_kernel, out_shape=(jax.ShapeDtypeStruct(initial_fiel...  0.97 us

profile of v4, /device:TPU:0, one launch (start us, length us, event | category | flops | bytes accessed | tf_op | source)
XLA Modules:
  0.0 32.4 jit_solution(16515611356921423256)
XLA Ops:
  0.6 30.8 %shard_map.86 = (f32[3,8,32,128]{3,2,1,0:T(8,128)S(1)}, f32[20,512]{1,0:T(8,128)S(1)}) custom-call(f32[3,8,32,128]{3,2,1,0:T(8,128)} %field_ref.1, f32[8,32,128]{2,1,0:T(8,128)} %perm_ref.1, bf16[12,24,256]{2,1,0:T(8,128)(2,1)} %bitcast.4, s32[1,24]{1,0:T(1,128)} %bitcast.5, s32[1,24]{1,0:T(1,128)} %bitcast.6, s32[24,4096]{1,0:T(8,128)} %delays_hbm.1, ...), custom_call_target="tpu_custom_call" | custom-call | tf_op jit(solution)/shard_map/pallas_call | solution.py:608
  31.4 1.0 %shard_map.87 = (f32[3,8,32,128]{3,2,1,0:T(8,128)}, f32[20,1,512]{2,1,0:T(1,128)}) custom-call(f32[3,8,32,128]{3,2,1,0:T(8,128)S(1)} %get-tuple-element.6.e_ref, f32[20,512]{1,0:T(8,128)S(1)} %get-tuple-element.7.far_ref), custom_call_target="tpu_custom_call" | custom-call | tf_op jit(solution)/shard_map/pallas_call | solution.py:623
